TPU v7x, 512 devices: a whole 4x8x8 slice. The times are simulated.
512 devices in a mesh: expert: 128 (over y, z, core), dp: 4 (over x).
Axes of the slice: x: 4, y: 8, z: 8, core: 2. Of those that a mesh axis runs over, the one named last changes fastest.
Arguments:
- hidden: bfloat16 [128, 4, 256, 1024], P('expert', 'dp'), may hold values from -6 to 6
- w_down: bfloat16 [128, 1024, 3584], P('expert', 'dp'), may hold values from -0.1875 to 0.1875
- expert_ids: int32 [4, 2048, 8], P('dp', 'expert'), may hold values from 0 to 127, all different within a row; in each aligned block of 16 rows (0 to 15, 16 to 31, ..., all dimensions but the last counted through in order) at most 2 rows name the same one
- route_weights: float32 [4, 2048, 8], P('dp', 'expert'), may hold values from 0.1 to 0.6
- grad_out: bfloat16 [4, 2048, 3584], P('dp', 'expert'), may hold values from -6 to 6
Outputs:
- mixed: bfloat16 [4, 2048, 3584], P('dp', 'expert')
- d_hidden: bfloat16 [128, 4, 256, 1024], P('expert', 'dp')
- d_w_down: bfloat16 [128, 1024, 3584], P('expert', 'dp')
- d_route: float32 [4, 2048, 8], P('dp', 'expert')
Inputs may be any that keep to these rules, and one draw needn't show every extreme that they name: `expert_ids`: among the 16 tokens of one device no expert is chosen more than 2 times, and some expert is chosen exactly 2 times; the 8 choices of a token are distinct.
All inputs are finite; a program needn't handle non-finite values.
Results may differ from a plain program's by a relative error of at most 0.0085.
Values may be sent and summed in bfloat16 or wider, within the bound.
A program may use at most 128 MiB of HBM per device.

v0:
```python
import jax
import jax.numpy as jnp
from jax import lax
from jax.sharding import PartitionSpec as P


def slot_ranks(choices, experts):
    flat = choices.reshape(-1)
    onehot = (flat[:, None] == jnp.arange(experts, dtype=jnp.int32)[None, :]).astype(jnp.int32)
    earlier = jnp.cumsum(onehot, axis=0) - onehot
    return jnp.sum(earlier * onehot, axis=1).reshape(choices.shape)


def on_device(hidden, w_down, expert_ids, route_weights, grad_out):
    experts = lax.axis_size("expert")
    groups = lax.axis_size("dp")
    slots = hidden.shape[2] // experts
    width = w_down.shape[2]
    w_whole = lax.all_gather(w_down, "dp", axis=1, tiled=True)[0]
    out_slots = jnp.dot(hidden[0, 0], w_whole, preferred_element_type=jnp.float32).astype(
        jnp.bfloat16
    )
    arrived = lax.all_to_all(
        out_slots.reshape(experts, slots, width), "expert", split_axis=0, concat_axis=0, tiled=True
    )
    arrived = arrived.reshape(experts * slots, width)
    choices = expert_ids[0]
    weights = route_weights[0]
    cotangent = grad_out[0].astype(jnp.float32)
    rows = choices * slots + slot_ranks(choices, experts)
    out_pair = arrived[rows].astype(jnp.float32)
    mixed = jnp.einsum("tk,tkd->td", weights, out_pair)
    d_route = jnp.einsum("td,tkd->tk", cotangent, out_pair)
    grad_pair = (weights[..., None] * cotangent[:, None, :]).astype(jnp.bfloat16)
    outgoing = jnp.zeros((experts * slots, width), jnp.bfloat16)
    outgoing = outgoing.at[rows.reshape(-1)].set(grad_pair.reshape(-1, width))
    mine = lax.all_to_all(
        outgoing.reshape(experts, 1, slots, width),
        "expert",
        split_axis=0,
        concat_axis=0,
        tiled=True,
    )
    own_grads = mine[:, 0]
    slot_grads = lax.all_gather(mine, "dp", axis=1, tiled=True)
    d_hidden = jnp.einsum(
        "rd,hd->rh", own_grads.reshape(-1, width), w_whole, preferred_element_type=jnp.float32
    ).astype(jnp.bfloat16)
    columns = lax.all_to_all(hidden, "dp", split_axis=3, concat_axis=1, tiled=True)[0]
    columns = columns.reshape(groups, experts, slots, columns.shape[-1])
    d_weight = jnp.einsum(
        "gsch,sgcd->hd", columns, slot_grads, preferred_element_type=jnp.float32
    ).astype(jnp.bfloat16)
    return (
        mixed.astype(jnp.bfloat16)[None],
        d_hidden.reshape(hidden.shape),
        d_weight[None],
        d_route[None],
    )


def solution(mesh):
    placed = (
        P("expert", "dp", None, None),
        P("expert", "dp", None),
        P("dp", "expert", None),
        P("dp", "expert", None),
        P("dp", "expert", None),
    )
    return jax.shard_map(
        on_device,
        mesh=mesh,
        in_specs=placed,
        out_specs=(
            P("dp", "expert", None),
            P("expert", "dp", None, None),
            P("expert", "dp", None),
            P("dp", "expert", None),
        ),
        check_vma=False,
    )
```

profile of v0, /device:TPU:1, one launch (start us, length us, event | category | flops | bytes accessed | tf_op | source)
XLA Modules:
  0.0 197.7 jit_solution(9017277390061045914)
XLA Ops:
  7.2 0.7 all-gather.3.cloned.1.call-update
  9.0 2.5 %scatter_custom_fusion = bf16[256,3584]{1,0:T(8,128)(2,1)S(1)} fusion(s32[128]{0:T(128)S(1)} %fusion.30, f32[16,3584]{1,0:T(8,128)S(1)} %bitcast_convert_fusion.1, f32[128]{0:T(128)S(1)} %mul.53, bf16[]{:T(256)} %constant.7.clone.1), kind=kCustom, calls=%fused_computation.14 | custom fusion | flops 917504 | bytes 2064898 | tf_op jit(solution)/shard_map/scatter | solution.py:36
  11.5 1.6 reshape.99
  13.2 64.9 %all_to_all.25 = bf16[128,1,2,3584]{3,2,1,0:T(2,128)(2,1)S(1)} all-to-all(bf16[128,1,2,3584]{3,2,1,0:T(2,128)(2,1)} %bitcast.75), channel_id=1, replica_groups=mesh['expert'=128,'dp'=4] {'expert'}, dimensions={0} | all-to-all | bytes 3670016 | tf_op jit(solution)/shard_map/all_to_all | solution.py:37
  78.1 3.7 %copy.52 = bf16[128,1,2,3584]{0,3,1,2:T(8,128)(2,1)} copy(bf16[128,1,2,3584]{3,2,1,0:T(2,128)(2,1)S(1)} %all_to_all.25) | data formatting | bytes 3670016 | tf_op jit(solution)/shard_map/all_to_all | solution.py:37
  81.8 1.0 copy-done
  82.8 0.8 copy.53
  84.2 3.8 %reduce = bf16[1024,256]{1,0:T(8,128)(2,1)S(1)} reduce(bf16[1024,1,1,256]{3,2,1,0:T(2,128)(2,1)S(1)} %bitcast.77, bf16[]{:T(256)} %broadcast.58), dimensions={1,2}, to_apply=%bitcast.68.reduce_sub_computation | reduce | bytes 1048578
  88.0 0.9 reshape.125
  88.9 4.0 %all-to-all-start.2 = ((bf16[4,2,32768]{2,1,0:T(2,128)(2,1)}), bf16[4,2,32768]{2,1,0:T(2,128)(2,1)S(1)}, u32[]{:S(2)}, u32[]{:S(2)}) async-start(bf16[4,2,32768]{2,1,0:T(2,128)(2,1)} %reshape.125), calls=%async_computation.2 | async-start | bytes 1048576 | tf_op jit(solution)/shard_map/all_to_all | solution.py:49
  93.0 2.2 %all-gather.3.cloned.1.call-done = bf16[1,1024,3584]{2,1,0:T(8,128)(2,1)} async-done(((bf16[1,256,3584]{2,1,0:T(8,128)(2,1)}), bf16[1,1024,3584]{2,1,0:T(8,128)(2,1)}) %all-gather.3.cloned.1.call-update) | async-done | bytes 7340048 | tf_op jit(solution)/shard_map/all_gather | solution.py:19
  95.1 6.4 %fusion.5 = bf16[256,3584]{1,0:T(8,128)(2,1)} fusion(bf16[1,1024,3584]{2,1,0:T(8,128)(2,1)} %all-gather.3.cloned.1.call-done, bf16[1,1,256,1024]{3,2,1,0:T(8,128)(2,1)S(1)} %copy-done.1), kind=kOutput, calls=%fused_computation.8 | convolution fusion | flops 1879965696 | bytes 9699328 | tf_op jit(solution)/shard_map/dot_general | solution.py:20
  101.5 4.7 %reshape.96 = bf16[128,2,3584]{2,1,0:T(2,128)(2,1)} reshape(bf16[256,3584]{1,0:T(8,128)(2,1)} %fusion.5) | data formatting | bytes 3670016 | tf_op jit(solution)/shard_map/reshape | solution.py:24
  106.2 20.2 %all-to-all-start = ((bf16[128,2,3584]{2,1,0:T(2,128)(2,1)}), bf16[128,2,3584]{2,1,0:T(2,128)(2,1)}, u32[]{:S(2)}, u32[]{:S(2)}) async-start(bf16[128,2,3584]{2,1,0:T(2,128)(2,1)} %reshape.96), calls=%async_computation | async-start | bytes 3670016 | tf_op jit(solution)/shard_map/all_to_all | solution.py:23
  127.8 1.6 reshape_squeeze.6
  129.5 6.6 %fusion.13 = bf16[1,1,256,1024]{3,2,1,0:T(8,128)(2,1)} fusion(bf16[256,3584]{1,0:T(8,128)(2,1)} %reshape_squeeze.6, bf16[1,1024,3584]{2,1,0:T(8,128)(2,1)} %all-gather.3.cloned.1.call-done), kind=kOutput, calls=%fused_computation.13 | convolution fusion | flops 1879310336 | bytes 9699328 | tf_op jit(solution)/shard_map/rd,hd->rh/dot_general | solution.py:46
  136.1 36.5 %all-to-all-done = bf16[128,2,3584]{2,1,0:T(2,128)(2,1)} async-done(((bf16[128,2,3584]{2,1,0:T(2,128)(2,1)}), bf16[128,2,3584]{2,1,0:T(2,128)(2,1)}, u32[]{:S(2)}, u32[]{:S(2)}) %all-to-all-start) | async-done | bytes 1835040 | tf_op jit(solution)/shard_map/all_to_all | solution.py:23
  172.6 4.1 %reshape.97 = bf16[256,3584]{1,0:T(8,128)(2,1)S(1)} reshape(bf16[128,2,3584]{2,1,0:T(2,128)(2,1)} %all-to-all-done) | data formatting | bytes 3670016 | tf_op jit(solution)/shard_map/reshape | solution.py:26
  176.7 1.1 gather_fusion
  178.2 0.7 copy.70
  179.5 0.7 copy.61
  180.2 3.0 %all-gather.5.cloned.1.call-done = bf16[128,4,2,3584]{0,3,1,2:T(8,128)(2,1)} async-done(((bf16[128,1,2,3584]{0,3,1,2:T(8,128)(2,1)}), bf16[128,4,2,3584]{0,3,1,2:T(8,128)(2,1)}) %all-gather.5.cloned.1.call-update) | async-done | bytes 7340048 | tf_op jit(solution)/shard_map/all_gather | solution.py:45
  183.1 5.2 %fusion.8 = bf16[1,256,3584]{1,2,0:T(8,128)(2,1)S(1)} fusion(bf16[128,4,2,3584]{0,3,1,2:T(8,128)(2,1)} %all-gather.5.cloned.1.call-done, bf16[4,128,2,256]{3,0,2,1:T(4,128)(2,1)S(1)} %bitcast.79), kind=kOutput, calls=%fused_computation.9 | convolution fusion | flops 1879965696 | bytes 9699328 | tf_op jit(solution)/shard_map/gsch,sgcd->hd/dot_general | solution.py:51
  188.3 2.6 %copy.56 = bf16[1,256,3584]{2,1,0:T(8,128)(2,1)} copy(bf16[1,256,3584]{1,2,0:T(8,128)(2,1)S(1)} %fusion.8) | data formatting | bytes 3670016
  (38 shorter events, 3.9 us)
Async XLA Ops:
  7.2 0.8 copy-start.3
  7.2 1.1 copy-start.4
  7.2 1.8 copy-start.2
  7.2 87.9 %all-gather.3.cloned.1.call-start = ((), (), s32[]{:S(2)}) async-start(), calls=%async_computation.3 | async-start | bytes 9175040 | tf_op jit(solution)/shard_map/all_gather | solution.py:19
  7.9 175.2 %all-gather.5.cloned.1.call-start = ((), (), s32[]{:S(2)}) async-start(), calls=%async_computation.4 | async-start | bytes 9175040 | tf_op jit(solution)/shard_map/all_gather | solution.py:45
  81.8 1.0 copy-start
  88.0 7.1 %copy-start.1 = (bf16[1,1,256,1024]{3,2,1,0:T(8,128)(2,1)S(1)}, bf16[1,1,256,1024]{3,2,1,0:T(8,128)(2,1)}, u32[]{:S(2)}) copy-start(bf16[1,1,256,1024]{3,2,1,0:T(8,128)(2,1)} %param.5) | copy-start | bytes 1572868
  88.9 17.3 %all-to-all-start.2 = ((bf16[4,2,32768]{2,1,0:T(2,128)(2,1)}), bf16[4,2,32768]{2,1,0:T(2,128)(2,1)S(1)}, u32[]{:S(2)}, u32[]{:S(2)}) async-start(bf16[4,2,32768]{2,1,0:T(2,128)(2,1)} %reshape.125), calls=%async_computation.2 | async-start | bytes 1048576 | tf_op jit(solution)/shard_map/all_to_all | solution.py:49
  106.2 66.4 %all-to-all-start = ((bf16[128,2,3584]{2,1,0:T(2,128)(2,1)}), bf16[128,2,3584]{2,1,0:T(2,128)(2,1)}, u32[]{:S(2)}, u32[]{:S(2)}) async-start(bf16[128,2,3584]{2,1,0:T(2,128)(2,1)} %reshape.96), calls=%async_computation | async-start | bytes 3670016 | tf_op jit(solution)/shard_map/all_to_all | solution.py:23
Sparse Core Ops, SparseCore 0:
  10.1 84.9 all-gather.2
  97.2 85.8 all-gather.4
where the time goes:
time: 198 us
  blocking collectives  64.9 us (33%)
  waiting for transfers between devices  42.3 us (21%)
  local copies, waits for them, and re-layouts  25.9 us (13%)
  starting transfers between devices  24.3 us (12%)
  matrix products  19.2 us (10%)
  between operations  14.2 us (7%)
  other arithmetic  6.83 us (3%)
    all_to_all x1, blocking collectives, on_device(): lax.all_to_all(outgoing.reshape(experts, 1, slots, width), 'expert', spli...  64.9 us
    all_to_all x1, waiting for transfers between devices, on_device(): lax.all_to_all(out_slots.reshape(experts, slots, width), 'expert', split_...  36.5 us
    all_to_all x1, starting transfers between devices, on_device(): lax.all_to_all(out_slots.reshape(experts, slots, width), 'expert', split_...  20.2 us
    dot_general x1, matrix products, on_device(): jnp.einsum('rd,hd->rh', own_grads.reshape(-1, width), w_whole, preferred_...  6.64 us
    unnamed x18, local copies, waits for them, and re-layouts  6.64 us
    dot_general x1, matrix products, on_device(): jnp.dot(hidden[0, 0], w_whole, preferred_element_type=jnp.float32)  6.37 us
    dot_general x1, matrix products, on_device(): jnp.einsum('gsch,sgcd->hd', columns, slot_grads, preferred_element_type=j...  5.17 us
    reshape x1, local copies, waits for them, and re-layouts, on_device(): out_slots.reshape(experts, slots, width)  4.75 us
  transfers between devices with their start and end apart: 4, of which 3 were waited for; matrix products, arithmetic and copies ran while one was open for 22% of the time, Pallas kernels for 0%

commit v1 on v0

--- a/solution.py
+++ b/solution.py
@@ -46,7 +46,10 @@
     d_hidden = jnp.einsum(
         "rd,hd->rh", own_grads.reshape(-1, width), w_whole, preferred_element_type=jnp.float32
     ).astype(jnp.bfloat16)
-    columns = lax.all_to_all(hidden, "dp", split_axis=3, concat_axis=1, tiled=True)[0]
+    columns = jnp.concatenate(
+        lax.all_to_all(jnp.stack(jnp.split(hidden, lax.axis_size("dp"), axis=3)), "dp", 0, 0),
+        axis=1,
+    )[0]
     columns = columns.reshape(groups, experts, slots, columns.shape[-1])
     d_weight = jnp.einsum(
         "gsch,sgcd->hd", columns, slot_grads, preferred_element_type=jnp.float32

time: 198 us -> 197 us (level)
  waiting for transfers between devices: 42.3 us -> 55.5 us
  local copies, waits for them, and re-layouts: 25.9 us -> 18.3 us
  starting transfers between devices: 24.3 us -> 19.5 us
  other arithmetic: 6.83 us -> 3.87 us
    all_gather x1, waiting for transfers between devices: 2.16 us -> 14.8 us  [on_device(): w_whole = lax.all_gather(w_down, 'dp', axis=1, tiled=True)[0]]
    unnamed x18 -> x10, local copies, waits for them, and re-layouts: 6.64 us -> 1.17 us
    all_to_all x1, starting transfers between devices: 20.2 us -> 15.4 us  [on_device(): lax.all_to_all(out_slots.reshape(experts, slots, width), 'expert', split_...]
    unnamed x1 -> x0, other arithmetic: 3.82 us -> none
    all_to_all x1, local copies, waits for them, and re-layouts: 3.72 us -> 1.42 us  [on_device(): lax.all_to_all(outgoing.reshape(experts, 1, slots, width), 'expert', spli...]
  transfers between devices with their start and end apart: 4 -> 4, of which waited for: 3 -> 3; matrix products, arithmetic and copies ran while one was open for 22% -> 18% of each run, Pallas kernels for 0% -> 0%
where the time goes in v1:
time: 197 us
  blocking collectives  64.9 us (33%)
  waiting for transfers between devices  55.5 us (28%)
  matrix products  20.4 us (10%)
  starting transfers between devices  19.5 us (10%)
  local copies, waits for them, and re-layouts  18.3 us (9%)
  between operations  14.2 us (7%)
  other arithmetic  3.87 us (2%)
    all_to_all x1, blocking collectives, on_device(): lax.all_to_all(outgoing.reshape(experts, 1, slots, width), 'expert', spli...  64.9 us
    all_to_all x1, waiting for transfers between devices, on_device(): lax.all_to_all(out_slots.reshape(experts, slots, width), 'expert', split_...  37 us
    all_to_all x1, starting transfers between devices, on_device(): lax.all_to_all(out_slots.reshape(experts, slots, width), 'expert', split_...  15.4 us
    all_gather x1, waiting for transfers between devices, on_device(): w_whole = lax.all_gather(w_down, 'dp', axis=1, tiled=True)[0]  14.8 us
    dot_general x1, matrix products, on_device(): jnp.einsum('rd,hd->rh', own_grads.reshape(-1, width), w_whole, preferred_...  6.67 us
    dot_general x1, matrix products, on_device(): jnp.einsum('gsch,sgcd->hd', columns, slot_grads, preferred_element_type=j...  6.41 us
    dot_general x1, matrix products, on_device(): jnp.dot(hidden[0, 0], w_whole, preferred_element_type=jnp.float32)  6.37 us
    reshape x1, local copies, waits for them, and re-layouts, on_device(): out_slots.reshape(experts, slots, width)  4.75 us
  transfers between devices with their start and end apart: 4, of which 3 were waited for; matrix products, arithmetic and copies ran while one was open for 18% of the time, Pallas kernels for 0%

profile of v1, /device:TPU:1, one launch (start us, length us, event | category | flops | bytes accessed | tf_op | source)
XLA Modules:
  0.0 196.7 jit_solution(11578618305341478751)
XLA Ops:
  7.2 0.7 all-gather.3.cloned.1.call-update
  9.0 2.5 %scatter_custom_fusion = bf16[256,3584]{1,0:T(8,128)(2,1)S(1)} fusion(s32[128]{0:T(128)S(1)} %fusion.30, f32[16,3584]{1,0:T(8,128)S(1)} %bitcast_convert_fusion.1, f32[128]{0:T(128)S(1)} %mul.53, bf16[]{:T(256)} %constant.7.clone.1), kind=kCustom, calls=%fused_computation.14 | custom fusion | flops 917504 | bytes 2064898 | tf_op jit(solution)/shard_map/scatter | solution.py:36
  11.5 1.6 reshape.98
  13.2 64.9 %all_to_all.15 = bf16[128,1,2,3584]{3,2,1,0:T(2,128)(2,1)S(1)} all-to-all(bf16[128,1,2,3584]{3,2,1,0:T(2,128)(2,1)} %bitcast.76), channel_id=1, replica_groups=mesh['expert'=128,'dp'=4] {'expert'}, dimensions={0} | all-to-all | bytes 3670016 | tf_op jit(solution)/shard_map/all_to_all | solution.py:37
  78.1 1.4 copy.39
  79.5 1.0 copy-done
  80.6 0.9 pad_maximum_fusion
  81.4 4.0 %all-to-all-start.2 = ((bf16[4,1,1,256,256]{4,3,2,1,0:T(8,128)(2,1)}), bf16[4,1,1,256,256]{4,3,2,1,0:T(8,128)(2,1)S(1)}, u32[]{:S(2)}, u32[]{:S(2)}) async-start(bf16[4,1,1,256,256]{4,3,2,1,0:T(8,128)(2,1)} %pad_maximum_fusion), calls=%async_computation.2 | async-start | bytes 1048576 | tf_op jit(solution)/shard_map/all_to_all | solution.py:50
  85.4 14.8 %all-gather.3.cloned.1.call-done = bf16[1,1024,3584]{2,1,0:T(8,128)(2,1)} async-done(((bf16[1,256,3584]{2,1,0:T(8,128)(2,1)}), bf16[1,1024,3584]{2,1,0:T(8,128)(2,1)}) %all-gather.3.cloned.1.call-update) | async-done | bytes 7340048 | tf_op jit(solution)/shard_map/all_gather | solution.py:19
  100.2 6.4 %fusion.5 = bf16[256,3584]{1,0:T(8,128)(2,1)} fusion(bf16[1,1024,3584]{2,1,0:T(8,128)(2,1)} %all-gather.3.cloned.1.call-done, bf16[1,1,256,1024]{3,2,1,0:T(8,128)(2,1)S(1)} %copy-done), kind=kOutput, calls=%fused_computation.8 | convolution fusion | flops 1879965696 | bytes 9699328 | tf_op jit(solution)/shard_map/dot_general | solution.py:20
  106.6 4.8 %reshape.95 = bf16[128,2,3584]{2,1,0:T(2,128)(2,1)} reshape(bf16[256,3584]{1,0:T(8,128)(2,1)} %fusion.5) | data formatting | bytes 3670016 | tf_op jit(solution)/shard_map/reshape | solution.py:24
  111.3 15.4 %all-to-all-start = ((bf16[128,2,3584]{2,1,0:T(2,128)(2,1)}), bf16[128,2,3584]{2,1,0:T(2,128)(2,1)}, u32[]{:S(2)}, u32[]{:S(2)}) async-start(bf16[128,2,3584]{2,1,0:T(2,128)(2,1)} %reshape.95), calls=%async_computation | async-start | bytes 3670016 | tf_op jit(solution)/shard_map/all_to_all | solution.py:23
  127.2 0.4 copy.38
  127.6 1.6 reshape_squeeze.3
  129.2 6.7 %fusion.13 = bf16[1,1,256,1024]{3,2,1,0:T(8,128)(2,1)} fusion(bf16[256,3584]{1,0:T(8,128)(2,1)} %reshape_squeeze.3, bf16[1,1024,3584]{2,1,0:T(8,128)(2,1)} %all-gather.3.cloned.1.call-done), kind=kOutput, calls=%fused_computation.13 | convolution fusion | flops 1879310336 | bytes 9699328 | tf_op jit(solution)/shard_map/rd,hd->rh/dot_general | solution.py:46
  135.9 37.0 %all-to-all-done = bf16[128,2,3584]{2,1,0:T(2,128)(2,1)} async-done(((bf16[128,2,3584]{2,1,0:T(2,128)(2,1)}), bf16[128,2,3584]{2,1,0:T(2,128)(2,1)}, u32[]{:S(2)}, u32[]{:S(2)}) %all-to-all-start) | async-done | bytes 1835040 | tf_op jit(solution)/shard_map/all_to_all | solution.py:23
  172.9 4.1 %reshape.96 = bf16[256,3584]{1,0:T(8,128)(2,1)S(1)} reshape(bf16[128,2,3584]{2,1,0:T(2,128)(2,1)} %all-to-all-done) | data formatting | bytes 3670016 | tf_op jit(solution)/shard_map/reshape | solution.py:26
  177.0 1.1 gather_fusion
  178.1 0.4 fusion.18
  178.5 0.7 copy.53
  179.2 0.6 fusion.20
  179.7 0.7 copy.45
  180.4 3.0 %all-gather.5.cloned.1.call-done = bf16[128,4,2,3584]{3,0,1,2:T(8,128)(2,1)} async-done(((bf16[128,1,2,3584]{3,0,1,2:T(8,128)(2,1)}), bf16[128,4,2,3584]{3,0,1,2:T(8,128)(2,1)}) %all-gather.5.cloned.1.call-update) | async-done | bytes 7340048 | tf_op jit(solution)/shard_map/all_gather | solution.py:45
  183.4 6.4 %fusion.8 = bf16[1,256,3584]{2,1,0:T(8,128)(2,1)} fusion(bf16[128,4,2,3584]{3,0,1,2:T(8,128)(2,1)} %all-gather.5.cloned.1.call-done, bf16[4,128,2,256]{3,0,2,1:T(4,128)(2,1)S(1)} %bitcast.77), kind=kOutput, calls=%fused_computation.9 | convolution fusion | flops 1879965696 | bytes 9699328 | tf_op jit(solution)/shard_map/gsch,sgcd->hd/dot_general | solution.py:54
  (31 shorter events, 1.5 us)
Async XLA Ops:
  7.2 0.8 copy-start.2
  7.2 1.1 copy-start.3
  7.2 1.8 copy-start.1
  7.2 93.0 %all-gather.3.cloned.1.call-start = ((), (), s32[]{:S(2)}) async-start(), calls=%async_computation.3 | async-start | bytes 9175040 | tf_op jit(solution)/shard_map/all_gather | solution.py:19
  7.9 175.5 %all-gather.5.cloned.1.call-start = ((), (), s32[]{:S(2)}) async-start(), calls=%async_computation.4 | async-start | bytes 9175040 | tf_op jit(solution)/shard_map/all_gather | solution.py:45
  79.5 1.0 copy-start
  81.4 29.9 %all-to-all-start.2 = ((bf16[4,1,1,256,256]{4,3,2,1,0:T(8,128)(2,1)}), bf16[4,1,1,256,256]{4,3,2,1,0:T(8,128)(2,1)S(1)}, u32[]{:S(2)}, u32[]{:S(2)}) async-start(bf16[4,1,1,256,256]{4,3,2,1,0:T(8,128)(2,1)} %pad_maximum_fusion), calls=%async_computation.2 | async-start | bytes 1048576 | tf_op jit(solution)/shard_map/all_to_all | solution.py:50
  111.3 61.6 %all-to-all-start = ((bf16[128,2,3584]{2,1,0:T(2,128)(2,1)}), bf16[128,2,3584]{2,1,0:T(2,128)(2,1)}, u32[]{:S(2)}, u32[]{:S(2)}) async-start(bf16[128,2,3584]{2,1,0:T(2,128)(2,1)} %reshape.95), calls=%async_computation | async-start | bytes 3670016 | tf_op jit(solution)/shard_map/all_to_all | solution.py:23
Sparse Core Ops, SparseCore 0:
  10.1 90.0 all-gather.2
  102.3 81.0 all-gather.4
